TPU v7x, 32 devices: a whole 2x2x4 slice. The times are simulated.
32 devices in a mesh: dp: 8 (over z, x), seq: 4 (over y, core).
Axes of the slice: x: 2, y: 2, z: 4, core: 2. Of those that a mesh axis runs over, the one named last changes fastest.
Arguments:
- layer_in: bfloat16 [8192, 2048], P(('dp', 'seq')), may hold values from -6 to 6
- out_grad: bfloat16 [8192, 2048], P(('dp', 'seq')), may hold values from -6 to 6
- seq_start: int32 [8, 4], P('dp'), may hold values from 0 to 1, as said below
- norm1_gain: bfloat16 [2048], P(('dp', 'seq')), may hold values from 0.25 to 1.75
- norm1_shift: bfloat16 [2048], P(('dp', 'seq')), may hold values from -3 to 3
- proj_in: bfloat16 [2048, 12288], P(('dp', 'seq')), may hold values from -0.125 to 0.125
- proj_out: bfloat16 [4096, 2048], P(('dp', 'seq')), may hold values from -0.125 to 0.125
- norm2_gain: bfloat16 [2048], P(('dp', 'seq')), may hold values from 0.25 to 1.75
- norm2_shift: bfloat16 [2048], P(('dp', 'seq')), may hold values from -3 to 3
- ffn_up: bfloat16 [2048, 4096], P(('dp', 'seq')), may hold values from -0.125 to 0.125
- ffn_down: bfloat16 [4096, 2048], P(('dp', 'seq')), may hold values from -0.125 to 0.125
Outputs:
- layer_out: bfloat16 [8192, 2048], P(('dp', 'seq'))
- in_grad: bfloat16 [8192, 2048], P(('dp', 'seq'))
- norm1_gain_grad: float32 [2048], P(('dp', 'seq'))
- norm1_shift_grad: float32 [2048], P(('dp', 'seq'))
- proj_in_grad: float32 [2048, 12288], P(('dp', 'seq'))
- proj_out_grad: float32 [4096, 2048], P(('dp', 'seq'))
- norm2_gain_grad: float32 [2048], P(('dp', 'seq'))
- norm2_shift_grad: float32 [2048], P(('dp', 'seq'))
- ffn_up_grad: float32 [2048, 4096], P(('dp', 'seq'))
- ffn_down_grad: float32 [4096, 2048], P(('dp', 'seq'))
Inputs may be any that keep to these rules, and one draw needn't show every extreme that they name: `seq_start`: each group's first block is 1, and a 1 stands only at even block indices, so every sequence covers an even number of blocks of 256 tokens.
All inputs are finite; a program needn't handle non-finite values.
Results may differ from a plain program's by a relative error of at most 0.014.
The roundings to bfloat16 on the way count: a program that leaves them out, or rounds other values in their place, can miss the bound.
Values may be sent and summed in bfloat16 or wider, within the bound.
No kernel may reach another device: no remote copies, remote signals or barrier semaphores. Data moves between devices by JAX's collectives and lax.ppermute only.
A program may use at most 336 MiB of HBM per device.

v0:
```python
import jax
import jax.numpy as jnp
from jax import lax
from jax.sharding import PartitionSpec as P

D = 2048
HEADS = 8
VD = 4096
DK = 256
DV = 512
BOTH = ("dp", "seq")
f32 = jnp.float32
bf16 = jnp.bfloat16


def layer_norm(rows, row_gain, row_shift):
    average = jnp.mean(rows, axis=-1, keepdims=True)
    centred = rows - average
    spread = jnp.mean(centred * centred, axis=-1, keepdims=True)
    return centred * lax.rsqrt(spread + 1e-05) * row_gain + row_shift


def gate_norm(gate_pre, retained):
    average = jnp.mean(retained, axis=-1, keepdims=True)
    centred = retained - average
    spread = jnp.maximum(jnp.mean(centred * centred, axis=-1, keepdims=True), 0.25)
    normed = centred * lax.rsqrt(spread + 1e-05)
    swish = gate_pre * jax.nn.sigmoid(gate_pre)
    return swish * normed


def gelu_exact(values):
    return jax.nn.gelu(values, approximate=False)


def rotate(heads_in, cosine, sine):
    half_width = heads_in.shape[-1] // 2
    first = heads_in[..., :half_width]
    second = heads_in[..., half_width:]
    return jnp.concatenate(
        [first * cosine - second * sine, first * sine + second * cosine], axis=-1
    )


def dot(a, b, dims):
    return lax.dot_general(a, b, (dims, ((), ())), preferred_element_type=f32)


def seq_bits(size):
    return [1 << b for b in range(size.bit_length() - 1)]


def swap_seq(x, bit):
    size = lax.axis_size("seq")
    return lax.ppermute(x, "seq", [(i, i ^ bit) for i in range(size)])


def gather_seq(x):
    size, me = (lax.axis_size("seq"), lax.axis_index("seq"))
    held = x[None]
    for bit in reversed(seq_bits(size)):
        other = swap_seq(held, bit)
        upper = me & bit != 0
        held = jnp.where(upper, jnp.stack([other, held]), jnp.stack([held, other]))
        held = held.reshape((-1,) + x.shape) if bit == size // 2 else held
        if bit != size // 2:
            held = jnp.swapaxes(held, 0, 1).reshape((-1,) + x.shape)
    return held


def scatter_seq(x):
    size, me = (lax.axis_size("seq"), lax.axis_index("seq"))
    held = x
    for bit in seq_bits(size):
        pairs = held.reshape((held.shape[0] // 2, 2) + held.shape[1:])
        mine = jnp.where(me & bit != 0, 1, 0)
        keep = lax.dynamic_index_in_dim(pairs, mine, 1, False)
        give = lax.dynamic_index_in_dim(pairs, 1 - mine, 1, False)
        held = keep.astype(f32) + swap_seq(give.astype(bf16), bit).astype(f32)
    return held[0]


def exchange_seq(x):
    return lax.all_to_all(x, "seq", 0, 0)


def gather_dp(x):
    return lax.all_gather(x, "dp", axis=0, tiled=True)


def scatter_dp(x):
    return lax.psum_scatter(x.astype(bf16), "dp", scatter_dimension=0, tiled=True)


def local(
    layer_in,
    out_grad,
    seq_start,
    norm1_gain,
    norm1_shift,
    proj_in,
    proj_out,
    norm2_gain,
    norm2_shift,
    ffn_up,
    ffn_down,
):
    S, G = (lax.axis_size("seq"), lax.axis_size("dp"))
    me = lax.axis_index("seq")
    T = layer_in.shape[0]
    TG = S * T
    H = HEADS // S
    QW, VW = (H * DK, H * DV)
    FR = ffn_down.shape[0]
    FW = G * FR
    norms = lax.all_gather(
        jnp.stack([norm1_gain, norm1_shift, norm2_gain, norm2_shift]), BOTH, axis=1, tiled=True
    ).astype(f32)
    gain_one, shift_one, gain_two, shift_two = norms
    rows_in = proj_in.shape[0]
    pieces = []
    start = 0
    for width in (QW, QW, VW, VW):
        part = proj_in[:, start : start + S * width]
        pieces.append(part.reshape(rows_in, S, width))
        start += S * width
    w_in = jnp.concatenate(pieces, axis=2).transpose(1, 0, 2)
    w_in = exchange_seq(w_in).reshape(S * rows_in, 2 * QW + 2 * VW)
    w_in = gather_dp(w_in)
    w_out = lax.ppermute(
        proj_out, BOTH, [(j * G + t, t * S + j) for j in range(S) for t in range(G)]
    )
    w_out = gather_dp(w_out)
    rows_up = ffn_up.shape[0]
    w_up = ffn_up.reshape(rows_up, G, S, FR).transpose(2, 0, 1, 3).reshape(S, rows_up, FW)
    w_up = gather_dp(exchange_seq(w_up).reshape(S * rows_up, FW))
    w_down = gather_dp(ffn_down)
    rows_full = layer_in.astype(f32)
    normed_one, norm1_back = jax.vjp(layer_norm, rows_full, gain_one, shift_one)
    hidden_one = gather_seq(normed_one.astype(bf16)).reshape(TG, D)
    cot = gather_seq(out_grad).reshape(TG, D)
    projected = dot(hidden_one, w_in, ((1,), (0,)))
    q_pre = projected[:, :QW].reshape(S, T, H, DK)
    k_pre = projected[:, QW : 2 * QW].reshape(S, T, H, DK)
    values = projected[:, 2 * QW : 2 * QW + VW].astype(bf16).reshape(S, T, H, DV)
    gate_pre = projected[:, 2 * QW + VW :].reshape(S, T, H, DV)
    half = DK // 2
    factor = jnp.power(10000.0, -jnp.arange(half, dtype=f32) / (half - 1))
    angles = jnp.arange(TG, dtype=f32)[:, None] * factor[None, :]
    cosine = jnp.cos(angles).reshape(S, T, 1, half)
    sine = jnp.sin(angles).reshape(S, T, 1, half)
    key_scale = DK ** (-0.5)
    queries = rotate(q_pre, cosine, sine).astype(bf16)
    keys = (rotate(k_pre, cosine, sine) * key_scale).astype(bf16)
    log_all = jnp.log(1.0 - jnp.exp2(-5.0 - jnp.arange(HEADS, dtype=f32)))
    log_decay = lax.dynamic_slice_in_dim(log_all, me * H, H)
    steps = jnp.arange(T, dtype=f32)
    decay_query = jnp.exp((steps + 1.0)[:, None] * log_decay[None, :])
    decay_key = jnp.exp((T - 1.0 - steps)[:, None] * log_decay[None, :])
    distance = steps[:, None] - steps[None, :]
    lower = distance[None] >= 0.0
    safe = jnp.where(lower, distance[None], 0.0)
    mask = jnp.where(lower, jnp.exp(safe * log_decay[:, None, None]), 0.0)
    block_decay = jnp.exp(T * log_decay)[:, None, None]
    keep = 1.0 - seq_start[0].astype(f32)
    query_decay = (queries.astype(f32) * decay_query[None, :, :, None]).astype(bf16)
    key_decay = (keys.astype(f32) * decay_key[None, :, :, None]).astype(bf16)

    def ein(spec, a, b):
        return jnp.einsum(spec, a, b, preferred_element_type=f32)

    raw = ein("bihd,bjhd->bhij", queries, keys)
    scores = (raw * mask[None]).astype(bf16)
    local_state = ein("bjhd,bjhe->bhde", key_decay, values)
    carry = jnp.zeros_like(local_state[0])
    states = []
    for b in range(S):
        state = keep[b] * carry
        states.append(state.astype(bf16))
        carry = block_decay * state + local_state[b]
    state_in = jnp.stack(states)
    retained = ein("bhij,bjhe->bihe", scores, values) + ein(
        "bihd,bhde->bihe", query_decay, state_in
    )
    gated, gate_back = jax.vjp(gate_norm, gate_pre, retained)
    mixed = gated.astype(bf16).reshape(TG, VW)
    attn = scatter_seq(dot(mixed, w_out, ((1,), (0,))).reshape(S, T, D))
    middle = rows_full + attn
    normed_two, norm2_back = jax.vjp(layer_norm, middle, gain_two, shift_two)
    hidden_two = gather_seq(normed_two.astype(bf16)).reshape(TG, D)
    up_pre = dot(hidden_two, w_up, ((1,), (0,)))
    active_full, gelu_back = jax.vjp(gelu_exact, up_pre)
    active = active_full.astype(bf16)
    down = scatter_seq(dot(active, w_down, ((1,), (0,))).reshape(S, T, D))
    layer_out = (middle + down).astype(bf16)
    down_grad = scatter_dp(dot(active, cot, ((0,), (0,)))).astype(f32)
    grad_active = dot(cot, w_down, ((1,), (1,)))
    grad_up = gelu_back(grad_active)[0].astype(bf16)
    up_grad = scatter_dp(dot(hidden_two, grad_up, ((0,), (0,))))
    up_grad = exchange_seq(up_grad.reshape(S, rows_up, FW)).reshape(S, rows_up, G, FR)
    up_grad = up_grad.transpose(1, 2, 0, 3).reshape(rows_up, G * S * FR).astype(f32)
    grad_hidden_two = scatter_seq(dot(grad_up, w_up, ((1,), (1,))).reshape(S, T, D))
    grad_mid_part, gain_two_grad, shift_two_grad = norm2_back(grad_hidden_two)
    grad_middle = out_grad.astype(f32) + grad_mid_part
    grad_attn = gather_seq(grad_middle.astype(bf16)).reshape(TG, D)
    out_term = scatter_dp(dot(mixed, grad_attn, ((0,), (0,))))
    out_grad_w = lax.ppermute(
        out_term, BOTH, [(t * S + j, j * G + t) for j in range(S) for t in range(G)]
    ).astype(f32)
    grad_mixed = dot(grad_attn, w_out, ((1,), (1,))).reshape(S, T, H, DV)
    grad_gate, grad_ret = gate_back(grad_mixed)
    grad_gate = grad_gate.astype(bf16)
    grad_ret = grad_ret.astype(bf16)
    grad_qdecay = ein("bihe,bhde->bihd", grad_ret, state_in)
    state_grad = ein("bihd,bihe->bhde", query_decay, grad_ret)
    grad_scores = ein("bihe,bjhe->bhij", grad_ret, values)
    grad_raw = (grad_scores * mask[None]).astype(bf16)
    later = jnp.zeros_like(state_grad[0])
    laters = [None] * S
    for b in reversed(range(S)):
        laters[b] = later.astype(bf16)
        later = keep[b] * (state_grad[b] + block_decay * later)
    grad_local = jnp.stack(laters)
    grad_query = (
        ein("bhij,bjhd->bihd", grad_raw, keys) + grad_qdecay * decay_query[None, :, :, None]
    )
    grad_key = (
        ein("bhij,bihd->bjhd", grad_raw, queries)
        + ein("bjhe,bhde->bjhd", values, grad_local) * decay_key[None, :, :, None]
    )
    grad_value = ein("bhij,bihe->bjhe", scores, grad_ret) + ein(
        "bjhd,bhde->bjhe", key_decay, grad_local
    )
    grad_qpre = rotate(grad_query, cosine, -sine).astype(bf16).reshape(TG, QW)
    grad_kpre = rotate(grad_key * key_scale, cosine, -sine).astype(bf16).reshape(TG, QW)
    grad_projected = jnp.concatenate(
        [grad_qpre, grad_kpre, grad_value.astype(bf16).reshape(TG, VW), grad_gate.reshape(TG, VW)],
        axis=1,
    )
    in_term = scatter_dp(dot(hidden_one, grad_projected, ((0,), (0,))))
    in_term = exchange_seq(in_term.reshape(S, rows_in, 2 * QW + 2 * VW))
    cols = []
    start = 0
    for width in (QW, QW, VW, VW):
        part = in_term[:, :, start : start + width]
        cols.append(part.transpose(1, 0, 2).reshape(rows_in, S * width))
        start += width
    in_grad_w = jnp.concatenate(cols, axis=1).astype(f32)
    grad_hidden_one = scatter_seq(dot(grad_projected, w_in, ((1,), (1,))).reshape(S, T, D))
    grad_in_part, gain_one_grad, shift_one_grad = norm1_back(grad_hidden_one)
    in_grad = (grad_middle + grad_in_part).astype(bf16)
    norm_grads = lax.psum_scatter(
        jnp.stack([gain_one_grad, shift_one_grad, gain_two_grad, shift_two_grad]),
        BOTH,
        scatter_dimension=1,
        tiled=True,
    )
    return (
        layer_out,
        in_grad,
        norm_grads[0],
        norm_grads[1],
        in_grad_w,
        out_grad_w,
        norm_grads[2],
        norm_grads[3],
        up_grad,
        down_grad,
    )


def solution(mesh):
    rows, vector = (P(BOTH, None), P(BOTH))
    in_specs = (rows, rows, P("dp", None), vector, vector, rows, rows, vector, vector, rows, rows)
    out_specs = (rows, rows, vector, vector, rows, rows, vector, vector, rows, rows)
    return jax.shard_map(local, mesh=mesh, in_specs=in_specs, out_specs=out_specs, check_vma=False)
```

profile of v0, /device:TPU:0, one launch (start us, length us, event | category | flops | bytes accessed | tf_op | source)
XLA Modules:
  0.0 1129.7 jit_solution(7035085313268230148)
XLA Ops:
  12.0 24.4 %all_to_all.20 = bf16[4,64,3072]{2,1,0:T(8,128)(2,1)} all-to-all(bf16[4,64,3072]{2,1,0:T(8,128)(2,1)S(1)} %copy.198), channel_id=1, replica_groups=mesh['dp'=8,'seq'=4] {'seq'}, dimensions={0} | all-to-all | bytes 3145728 | tf_op jit(solution)/shard_map/all_to_all | solution.py:84
  38.0 106.0 %all-gather = bf16[32,64,4]{1,2,0:T(4,128)(2,1)S(1)} all-gather(bf16[1,64,4]{1,2,0:T(4,128)(2,1)S(1)} %maximum_bitcast_fusion.1), channel_id=1, replica_groups=mesh['dp'=8,'seq'=4] {'dp','seq'}, dimensions={0}, use_global_device_ids=true | all-gather | bytes 16896 | tf_op jit(solution)/shard_map/all_gather | solution.py:116
  157.3 15.8 %collective-permute-done = bf16[1,256,2048]{2,1,0:T(8,128)(2,1)S(1)} collective-permute-done((bf16[1,256,2048]{2,1,0:T(8,128)(2,1)}, bf16[1,256,2048]{2,1,0:T(8,128)(2,1)S(1)}, u32[]{:S(2)}, u32[]{:S(2)}) %collective-permute-start) | collective-permute-done | bytes 1048608 | tf_op jit(solution)/shard_map/ppermute | solution.py:55
  188.4 51.1 %all-gather.6.cloned.1.call-done = bf16[2048,3072]{1,0:T(8,128)(2,1)} async-done(((bf16[256,3072]{1,0:T(8,128)(2,1)}), bf16[2048,3072]{1,0:T(8,128)(2,1)}) %all-gather.6.cloned.1.call-update) | async-done | bytes 12582928 | tf_op jit(solution)/shard_map/all_gather | solution.py:88
  239.5 17.0 %fusion.85 = f32[1024,3072]{1,0:T(8,128)S(1)} fusion(bf16[1024,2048]{1,0:T(8,128)(2,1)} %bitcast.265, bf16[2048,3072]{1,0:T(8,128)(2,1)} %all-gather.6.cloned.1.call-done), kind=kOutput, calls=%fused_computation.220 | convolution fusion | flops 12884901888 | bytes 29360128 | tf_op jit(solution)/shard_map/dot_general | solution.py:46
  270.5 6.7 reshape.732
  277.2 7.2 copy.200
  303.1 10.7 all-gather.8.cloned.1.call-done
  335.7 23.9 %collective-permute-done.4 = bf16[1,256,2048]{2,1,0:T(8,128)(2,1)} collective-permute-done((bf16[1,256,2048]{2,1,0:T(8,128)(2,1)S(1)}, bf16[1,256,2048]{2,1,0:T(8,128)(2,1)}, u32[]{:S(2)}, u32[]{:S(2)}) %collective-permute-start.4) | collective-permute-done | bytes 1048608 | tf_op jit(solution)/shard_map/ppermute | solution.py:55
  364.4 17.7 %collective-permute-done.9 = bf16[1,256,2048]{2,1,0:T(8,128)(2,1)S(1)} collective-permute-done((bf16[1,256,2048]{2,1,0:T(8,128)(2,1)}, bf16[1,256,2048]{2,1,0:T(8,128)(2,1)S(1)}, u32[]{:S(2)}, u32[]{:S(2)}) %collective-permute-start.9) | collective-permute-done | bytes 1048608 | tf_op jit(solution)/shard_map/ppermute | solution.py:55
  384.1 19.6 %collective-permute-done.5 = bf16[1,256,2048]{2,1,0:T(8,128)(2,1)S(1)} collective-permute-done((bf16[1,256,2048]{2,1,0:T(8,128)(2,1)S(1)}, bf16[1,256,2048]{2,1,0:T(8,128)(2,1)S(1)}, u32[]{:S(2)}, u32[]{:S(2)}) %collective-permute-start.5) | collective-permute-done | bytes 1048608 | tf_op jit(solution)/shard_map/ppermute | solution.py:55
  413.4 9.9 fusion.86
  423.2 38.1 %all-gather.12.cloned.1.call-done = bf16[1024,2048]{1,0:T(8,128)(2,1)} async-done(((bf16[128,2048]{1,0:T(8,128)(2,1)}), bf16[1024,2048]{1,0:T(8,128)(2,1)}) %all-gather.12.cloned.1.call-update) | async-done | bytes 4194320 | tf_op jit(solution)/shard_map/all_gather | solution.py:88
  461.3 16.9 %add_convert_fusion.2 = (bf16[1024,1024]{1,0:T(8,128)(2,1)S(1)}, f32[1024,1024]{1,0:T(8,128)S(1)}) fusion(f32[1024,1024]{1,0:T(8,128)} %fusion.86, bf16[1024,2048]{1,0:T(8,128)(2,1)} %bitcast.269, bf16[1024,2048]{1,0:T(8,128)(2,1)} %all-gather.12.cloned.1.call-done), kind=kOutput, calls=%fused_computation.31 | convolution fusion | flops 4370464768 | bytes 18874368 | tf_op jit(solution)/shard_map/dot_general | solution.py:46
  488.2 7.3 fusion.88
  510.5 18.6 %collective-permute-done.12 = bf16[1,256,2048]{2,1,0:T(8,128)(2,1)S(1)} collective-permute-done((bf16[1,256,2048]{2,1,0:T(8,128)(2,1)S(1)}, bf16[1,256,2048]{2,1,0:T(8,128)(2,1)S(1)}, u32[]{:S(2)}, u32[]{:S(2)}) %collective-permute-start.12) | collective-permute-done | bytes 1048608 | tf_op jit(solution)/shard_map/ppermute | solution.py:55
  529.9 21.3 %collective-permute-done.8 = bf16[1,256,2048]{2,1,0:T(8,128)(2,1)S(1)} collective-permute-done((bf16[1,256,2048]{2,1,0:T(8,128)(2,1)S(1)}, bf16[1,256,2048]{2,1,0:T(8,128)(2,1)S(1)}, u32[]{:S(2)}, u32[]{:S(2)}) %collective-permute-start.8) | collective-permute-done | bytes 1048608 | tf_op jit(solution)/shard_map/ppermute | solution.py:55
  557.0 23.3 %collective-permute-done.13 = bf16[1,256,2048]{2,1,0:T(8,128)(2,1)S(1)} collective-permute-done((bf16[1,256,2048]{2,1,0:T(8,128)(2,1)S(1)}, bf16[1,256,2048]{2,1,0:T(8,128)(2,1)S(1)}, u32[]{:S(2)}, u32[]{:S(2)}) %collective-permute-start.13) | collective-permute-done | bytes 1048608 | tf_op jit(solution)/shard_map/ppermute | solution.py:55
  653.1 16.0 %convolution_convert_fusion = bf16[2048,3072]{1,0:T(8,128)(2,1)} fusion(bf16[1024,2048]{1,0:T(8,128)(2,1)S(1)} %bitcast.266, bf16[1024,3072]{1,0:T(8,128)(2,1)S(1)} %constant_dynamic-update-slice_fusion), kind=kOutput, calls=%fused_computation | convolution fusion | flops 12891193344 | bytes 23068672 | tf_op jit(solution)/shard_map/dot_general | solution.py:46
  684.4 18.0 %fusion.90 = f32[1024,2048]{1,0:T(8,128)S(1)} fusion(bf16[1024,3072]{1,0:T(8,128)(2,1)} %copy-done.48, bf16[2048,3072]{1,0:T(8,128)(2,1)} %all-gather.6.cloned.1.call-done), kind=kOutput, calls=%fused_computation.225 | convolution fusion | flops 12884901888 | bytes 27262976 | tf_op jit(solution)/shard_map/dot_general | solution.py:46
  721.2 21.4 %all-to-all-done.3 = bf16[4,64,1024]{2,1,0:T(8,128)(2,1)} async-done(((bf16[4,64,1024]{2,1,0:T(8,128)(2,1)}), bf16[4,64,1024]{2,1,0:T(8,128)(2,1)}, u32[]{:S(2)}, u32[]{:S(2)}) %all-to-all-start.3) | async-done | bytes 524320 | tf_op jit(solution)/shard_map/all_to_all | solution.py:84
  752.4 133.5 %reduce-scatter.8.cloned.1.call-done = bf16[256,3072]{1,0:T(8,128)(2,1)} async-done(((bf16[2048,3072]{1,0:T(8,128)(2,1)}), bf16[256,3072]{1,0:T(8,128)(2,1)}) %reduce-scatter.8.cloned.1.call-update) | async-done | bytes 1572880 | tf_op jit(solution)/shard_map/reduce_scatter | solution.py:92
  894.2 82.5 %reduce-scatter.10.cloned.1.call-done = bf16[128,2048]{1,0:T(8,128)(2,1)} async-done(((bf16[1024,2048]{1,0:T(8,128)(2,1)}), bf16[128,2048]{1,0:T(8,128)(2,1)}) %reduce-scatter.10.cloned.1.call-update) | async-done | bytes 524304 | tf_op jit(solution)/shard_map/reduce_scatter | solution.py:92
  981.7 132.5 %reduce-scatter.16.cloned.1.call-done = f32[64,4]{1,0:T(8,128)} async-done(((f32[2048,4]{1,0:T(8,128)}), f32[64,4]{1,0:T(8,128)}) %reduce-scatter.16.cloned.1.call-update) | async-done | bytes 1040
  (361 shorter events, 274.1 us)
Async XLA Ops:
  7.2 232.3 %all-gather.6.cloned.1.call-start = ((), (), s32[]{:S(2)}) async-start(), calls=%async_computation.9 | async-start | bytes 14155776 | tf_op jit(solution)/shard_map/all_gather | solution.py:88
  36.4 277.4 %all-gather.8.cloned.1.call-start = ((), (), s32[]{:S(2)}) async-start(), calls=%async_computation.10 | async-start | bytes 4718592 | tf_op jit(solution)/shard_map/all_gather | solution.py:88
  146.9 26.2 %collective-permute-start = (bf16[1,256,2048]{2,1,0:T(8,128)(2,1)}, bf16[1,256,2048]{2,1,0:T(8,128)(2,1)S(1)}, u32[]{:S(2)}, u32[]{:S(2)}) collective-permute-start(bf16[1,256,2048]{2,1,0:T(8,128)(2,1)} %get-tuple-element.56), channel_id=1, source_target_pairs={{0,2},{1,3},{2,0},{3,1},{4,6},{5,7},{6,4},{7,5},{8,10},{9,11},{10,... | collective-permute-start | bytes 3145736 | tf_op jit(solution)/shard_map/ppermute | solution.py:55
  153.1 29.6 %all-to-all-start.1 = ((bf16[4,64,1024]{2,1,0:T(8,128)(2,1)}), bf16[4,64,1024]{2,1,0:T(8,128)(2,1)}, u32[]{:S(2)}, u32[]{:S(2)}) async-start(bf16[4,64,1024]{2,1,0:T(8,128)(2,1)} %reshape.737), calls=%async_computation.1 | async-start | bytes 1048576 | tf_op jit(solution)/shard_map/all_to_all | solution.py:84
  157.2 256.1 %all-gather.10.cloned.1.call-start = ((), (), s32[]{:S(2)}) async-start(), calls=%async_computation.11 | async-start | bytes 4718592 | tf_op jit(solution)/shard_map/all_gather | solution.py:88
  176.4 6.9 collective-permute-start.1
  182.7 278.6 %all-gather.12.cloned.1.call-start = ((), (), s32[]{:S(2)}) async-start(), calls=%async_computation.12 | async-start | bytes 4718592 | tf_op jit(solution)/shard_map/all_gather | solution.py:88
  333.5 26.2 %collective-permute-start.4 = (bf16[1,256,2048]{2,1,0:T(8,128)(2,1)S(1)}, bf16[1,256,2048]{2,1,0:T(8,128)(2,1)}, u32[]{:S(2)}, u32[]{:S(2)}) collective-permute-start(bf16[1,256,2048]{2,1,0:T(8,128)(2,1)S(1)} %dynamic-slice_convert_fusion.4), channel_id=1, source_target_pairs={{0,2},{1,3},{2,0},{3,1},{4,6},{5,7},{6,4},{7,5},{8,10},{9,11},{10,... | collective-permute-start | bytes 3145736 | tf_op jit(solution)/shard_map/ppermute | solution.py:55
  335.1 377.7 %reduce-scatter.12.cloned.1.call-start = ((), (), s32[]{:S(2)}) async-start(), calls=%async_computation.15 | async-start | bytes 4718592 | tf_op jit(solution)/shard_map/reduce_scatter | solution.py:92
  335.1 46.9 %collective-permute-start.9 = (bf16[1,256,2048]{2,1,0:T(8,128)(2,1)}, bf16[1,256,2048]{2,1,0:T(8,128)(2,1)S(1)}, u32[]{:S(2)}, u32[]{:S(2)}) collective-permute-start(bf16[1,256,2048]{2,1,0:T(8,128)(2,1)} %bitcast.42), channel_id=1, source_target_pairs={{0,2},{1,3},{2,0},{3,1},{4,6},{5,7},{6,4},{7,5},{8,10},{9,11},{10,... | collective-permute-start | bytes 3145736 | tf_op jit(solution)/shard_map/ppermute | solution.py:55
  362.9 40.9 %collective-permute-start.5 = (bf16[1,256,2048]{2,1,0:T(8,128)(2,1)S(1)}, bf16[1,256,2048]{2,1,0:T(8,128)(2,1)S(1)}, u32[]{:S(2)}, u32[]{:S(2)}) collective-permute-start(bf16[1,256,2048]{2,1,0:T(8,128)(2,1)S(1)} %fusion.126), channel_id=1, source_target_pairs={{0,2},{1,3},{2,0},{3,1},{4,6},{5,7},{6,4},{7,5},{8,10},{9,11},{10,... | collective-permute-start | bytes 3145736 | tf_op jit(solution)/shard_map/ppermute | solution.py:55
  384.0 22.1 %collective-permute-start.10 = (bf16[2,256,2048]{2,1,0:T(8,128)(2,1)S(1)}, bf16[2,256,2048]{2,1,0:T(8,128)(2,1)S(1)}, u32[]{:S(2)}, u32[]{:S(2)}) collective-permute-start(bf16[2,256,2048]{2,1,0:T(8,128)(2,1)S(1)} %maximum_select_fusion.8), channel_id=1, source_target_pairs={{0,1},{1,0},{2,3},{3,2},{4,5},{5,4},{6,7},{7,6},{8,9},{9,8},{10,11... | collective-permute-start | bytes 6291464 | tf_op jit(solution)/shard_map/ppermute | solution.py:55
  488.1 230.9 %reduce-scatter.14.cloned.1.call-start = ((), (), s32[]{:S(2)}) async-start(), calls=%async_computation.16 | async-start | bytes 4718592 | tf_op jit(solution)/shard_map/reduce_scatter | solution.py:92
  503.1 26.0 %collective-permute-start.12 = (bf16[1,256,2048]{2,1,0:T(8,128)(2,1)S(1)}, bf16[1,256,2048]{2,1,0:T(8,128)(2,1)S(1)}, u32[]{:S(2)}, u32[]{:S(2)}) collective-permute-start(bf16[1,256,2048]{2,1,0:T(8,128)(2,1)S(1)} %dynamic-slice_convert_fusion.2), channel_id=1, source_target_pairs={{0,2},{1,3},{2,0},{3,1},{4,6},{5,7},{6,4},{7,5},{8,10},{9,11},{10,... | collective-permute-start | bytes 3145736 | tf_op jit(solution)/shard_map/ppermute | solution.py:55
  509.0 42.2 %collective-permute-start.8 = (bf16[1,256,2048]{2,1,0:T(8,128)(2,1)S(1)}, bf16[1,256,2048]{2,1,0:T(8,128)(2,1)S(1)}, u32[]{:S(2)}, u32[]{:S(2)}) collective-permute-start(bf16[1,256,2048]{2,1,0:T(8,128)(2,1)S(1)} %dynamic-slice_convert_fusion.3), channel_id=1, source_target_pairs={{0,2},{1,3},{2,0},{3,1},{4,6},{5,7},{6,4},{7,5},{8,10},{9,11},{10,... | collective-permute-start | bytes 3145736 | tf_op jit(solution)/shard_map/ppermute | solution.py:55
  555.5 24.8 %collective-permute-start.13 = (bf16[1,256,2048]{2,1,0:T(8,128)(2,1)S(1)}, bf16[1,256,2048]{2,1,0:T(8,128)(2,1)S(1)}, u32[]{:S(2)}, u32[]{:S(2)}) collective-permute-start(bf16[1,256,2048]{2,1,0:T(8,128)(2,1)S(1)} %fusion.124), channel_id=1, source_target_pairs={{0,2},{1,3},{2,0},{3,1},{4,6},{5,7},{6,4},{7,5},{8,10},{9,11},{10,... | collective-permute-start | bytes 3145736 | tf_op jit(solution)/shard_map/ppermute | solution.py:55
  582.0 10.0 collective-permute-start.14
  588.5 297.4 %reduce-scatter.8.cloned.1.call-start = ((), (), s32[]{:S(2)}) async-start(), calls=%async_computation.13 | async-start | bytes 14155776 | tf_op jit(solution)/shard_map/reduce_scatter | solution.py:92
  669.1 307.6 %reduce-scatter.10.cloned.1.call-start = ((), (), s32[]{:S(2)}) async-start(), calls=%async_computation.14 | async-start | bytes 4718592 | tf_op jit(solution)/shard_map/reduce_scatter | solution.py:92
  711.3 34.6 %collective-permute-start.16 = (bf16[1,256,2048]{2,1,0:T(8,128)(2,1)}, bf16[1,256,2048]{2,1,0:T(8,128)(2,1)}, u32[]{:S(2)}, u32[]{:S(2)}) collective-permute-start(bf16[1,256,2048]{2,1,0:T(8,128)(2,1)} %dynamic-slice_convert_fusion.1), channel_id=1, source_target_pairs={{0,2},{1,3},{2,0},{3,1},{4,6},{5,7},{6,4},{7,5},{8,10},{9,11},{10,... | collective-permute-start | bytes 3145736 | tf_op jit(solution)/shard_map/ppermute | solution.py:55
  712.8 29.9 %all-to-all-start.3 = ((bf16[4,64,1024]{2,1,0:T(8,128)(2,1)}), bf16[4,64,1024]{2,1,0:T(8,128)(2,1)}, u32[]{:S(2)}, u32[]{:S(2)}) async-start(bf16[4,64,1024]{2,1,0:T(8,128)(2,1)} %bitcast.289), calls=%async_computation.6 | async-start | bytes 1048576 | tf_op jit(solution)/shard_map/all_to_all | solution.py:84
  716.9 397.3 %reduce-scatter.16.cloned.1.call-start = ((), (), s32[]{:S(2)}) async-start(), calls=%async_computation.17 | async-start | bytes 1081344
  885.9 232.7 %all-to-all-start.2 = ((bf16[4,64,3072]{2,1,0:T(8,128)(2,1)}), bf16[4,64,3072]{2,1,0:T(8,128)(2,1)}, u32[]{:S(2)}, u32[]{:S(2)}) async-start(bf16[4,64,3072]{2,1,0:T(8,128)(2,1)} %bitcast.286), calls=%async_computation.3 | async-start | bytes 3145728 | tf_op jit(solution)/shard_map/all_to_all | solution.py:84
  976.7 140.8 %collective-permute-start.17 = (bf16[128,2048]{1,0:T(8,128)(2,1)}, bf16[128,2048]{1,0:T(8,128)(2,1)S(1)}, u32[]{:S(2)}, u32[]{:S(2)}) collective-permute-start(bf16[128,2048]{1,0:T(8,128)(2,1)} %reduce-scatter.10.cloned.1.call-done), channel_id=1, source_target_pairs={{0,0},{4,1},{8,2},{12,3},{16,4},{20,5},{24,6},{28,7},{1,8},{5,9},{... | collective-permute-start | bytes 1572872 | tf_op jit(solution)/shard_map/ppermute | solution.py:207
  (81 other events, 1073.7 us)
Sparse Core Ops, SparseCore 0:
  36.5 202.9 all-gather.5
  242.2 71.5 all-gather.7
  315.9 71.6 all-gather.9
  389.6 71.6 all-gather.11
  488.3 86.3 reduce-scatter.11
  588.6 86.5 reduce-scatter.13
  678.8 206.9 reduce-scatter.7
  889.5 87.1 reduce-scatter.9
  979.6 134.5 reduce-scatter.15
where the time goes:
time: 1140 us; the launch traced here: 1130 us
  waiting for transfers between devices  620 us (54%)
  matrix products  131 us (11%)
  blocking collectives  130 us (11%)
  local copies, waits for them, and re-layouts  127 us (11%)
  other arithmetic  78 us (7%)
  starting transfers between devices  26.5 us (2%)
  between operations  16.3 us (1%)
    reduce_scatter x4, waiting for transfers between devices, scatter_dp(): lax.psum_scatter(x.astype(bf16), 'dp', scatter_dimension=0, tiled=True)  216 us
    ppermute x16, waiting for transfers between devices, swap_seq(): return lax.ppermute(x, 'seq', [(i, i ^ bit) for i in range(size)])  150 us
    unnamed x10, waiting for transfers between devices  133 us
    dot_general x12, matrix products, dot(): return lax.dot_general(a, b, (dims, ((), ())), preferred_element_type=f32)  120 us
    all_gather x1, blocking collectives, local(): lax.all_gather(jnp.stack([norm1_gain, norm1_shift, norm2_gain, norm2_shif...  106 us
    all_gather x4, waiting for transfers between devices, gather_dp(): return lax.all_gather(x, 'dp', axis=0, tiled=True)  99.8 us
    unnamed x166, local copies, waits for them, and re-layouts  45.7 us
    all_to_all x1, blocking collectives, exchange_seq(): return lax.all_to_all(x, 'seq', 0, 0)  24.4 us
  transfers between devices with their start and end apart: 30, of which 17 were waited for; matrix products, arithmetic and copies ran while one was open for 24% of the time, Pallas kernels for 0%

commit v1 on v0

--- a/solution.py
+++ b/solution.py
@@ -11,6 +11,22 @@
 BOTH = ("dp", "seq")
 f32 = jnp.float32
 bf16 = jnp.bfloat16
+
+
+def do_the_works(frame_in):
+    n_now, wide_out = (lax.axis_size("dp"), lax.axis_index("dp"))
+    o_now, local_next = (frame_in, 1)
+    while local_next < n_now:
+        v_next = lax.ppermute(
+            o_now,
+            axis_name="dp",
+            perm=tuple(((hop_no, hop_no ^ local_next) for hop_no in range(n_now))),
+        )
+        y1 = jnp.concatenate([o_now, v_next], axis=0)
+        block_last = jnp.concatenate([v_next, o_now], axis=0)
+        o_now = jnp.where(wide_out & local_next == 0, y1, block_last)
+        local_next = 2 * local_next
+    return o_now
 
 
 def layer_norm(rows, row_gain, row_shift):
@@ -85,7 +101,7 @@
 
 
 def gather_dp(x):
-    return lax.all_gather(x, "dp", axis=0, tiled=True)
+    return do_the_works(x)
 
 
 def scatter_dp(x):

time: 1140 us -> 1620 us (1.42)
  waiting for transfers between devices: 620 us -> 1030 us
  other arithmetic: 78 us -> 103 us
  blocking collectives: 130 us -> 151 us
    ppermute x0 -> x12, waiting for transfers between devices: none -> 526 us  [do_the_works(): lax.ppermute(o_now, axis_name='dp', perm=tuple(((hop_no, hop_no ^ local_n...]
    all_gather x4 -> x0, waiting for transfers between devices: 99.8 us -> none  [gather_dp(): return lax.all_gather(x, 'dp', axis=0, tiled=True)]
    ppermute x16, waiting for transfers between devices: 150 us -> 115 us  [swap_seq(): return lax.ppermute(x, 'seq', [(i, i ^ bit) for i in range(size)])]
    select_n x0 -> x9, other arithmetic: none -> 25.1 us  [do_the_works(): o_now = jnp.where(wide_out & local_next == 0, y1, block_last)]
    all_to_all x3, waiting for transfers between devices: 21.4 us -> 44.6 us  [exchange_seq(): return lax.all_to_all(x, 'seq', 0, 0)]
    all_gather x1, blocking collectives: 106 us -> 126 us  [local(): lax.all_gather(jnp.stack([norm1_gain, norm1_shift, norm2_gain, norm2_shif...]
    unnamed x166 -> x192, local copies, waits for them, and re-layouts: 45.7 us -> 47.8 us
    unnamed x10 -> x6, waiting for transfers between devices: 133 us -> 132 us
  transfers between devices with their start and end apart: 30 -> 38, of which waited for: 17 -> 22; matrix products, arithmetic and copies ran while one was open for 24% -> 14% of each run, Pallas kernels for 0% -> 0%
where the time goes in v1:
time: 1620 us; the launch traced here: 1610 us
  waiting for transfers between devices  1030 us (64%)
  blocking collectives  151 us (9%)
  matrix products  139 us (9%)
  local copies, waits for them, and re-layouts  128 us (8%)
  other arithmetic  103 us (6%)
  starting transfers between devices  40.6 us (3%)
  between operations  16.5 us (1%)
    ppermute x12, waiting for transfers between devices, do_the_works(): lax.ppermute(o_now, axis_name='dp', perm=tuple(((hop_no, hop_no ^ local_n...  526 us
    reduce_scatter x4, waiting for transfers between devices, scatter_dp(): lax.psum_scatter(x.astype(bf16), 'dp', scatter_dimension=0, tiled=True)  214 us
    unnamed x6, waiting for transfers between devices  132 us
    dot_general x12, matrix products, dot(): return lax.dot_general(a, b, (dims, ((), ())), preferred_element_type=f32)  128 us
    all_gather x1, blocking collectives, local(): lax.all_gather(jnp.stack([norm1_gain, norm1_shift, norm2_gain, norm2_shif...  126 us
    ppermute x16, waiting for transfers between devices, swap_seq(): return lax.ppermute(x, 'seq', [(i, i ^ bit) for i in range(size)])  115 us
    unnamed x192, local copies, waits for them, and re-layouts  47.8 us
    all_to_all x3, waiting for transfers between devices, exchange_seq(): return lax.all_to_all(x, 'seq', 0, 0)  44.6 us
  transfers between devices with their start and end apart: 38, of which 22 were waited for; matrix products, arithmetic and copies ran while one was open for 14% of the time, Pallas kernels for 0%

profile of v1, /device:TPU:0, one launch (start us, length us, event | category | flops | bytes accessed | tf_op | source)
XLA Modules:
  0.0 1610.1 jit_solution(9430246132014562789)
XLA Ops:
  11.9 24.1 %all_to_all.20 = bf16[4,64,3072]{2,1,0:T(8,128)(2,1)S(1)} all-to-all(bf16[4,64,3072]{2,1,0:T(8,128)(2,1)S(1)} %copy.198), channel_id=1, replica_groups=mesh['dp'=8,'seq'=4] {'seq'}, dimensions={0} | all-to-all | bytes 3145728 | tf_op jit(solution)/shard_map/all_to_all | solution.py:100
  37.5 34.3 %collective-permute-done.2 = bf16[256,3072]{1,0:T(8,128)(2,1)S(1)} collective-permute-done((bf16[256,3072]{1,0:T(8,128)(2,1)S(1)}, bf16[256,3072]{1,0:T(8,128)(2,1)S(1)}, u32[]{:S(2)}, u32[]{:S(2)}) %collective-permute-start.2) | collective-permute-done | bytes 1572896 | tf_op jit(solution)/shard_map/ppermute | solution.py:20
  77.6 126.5 %all-gather = bf16[32,64,4]{1,2,0:T(4,128)(2,1)S(1)} all-gather(bf16[1,64,4]{1,2,0:T(4,128)(2,1)S(1)} %maximum_bitcast_fusion.1), channel_id=1, replica_groups=mesh['dp'=8,'seq'=4] {'dp','seq'}, dimensions={0}, use_global_device_ids=true | all-gather | bytes 16896 | tf_op jit(solution)/shard_map/all_gather | solution.py:132
  204.0 9.9 maximum_select_fusion.1
  232.4 10.8 collective-permute-done
  247.8 124.4 %collective-permute-done.7 = bf16[256,2048]{1,0:T(8,128)(2,1)} collective-permute-done((bf16[256,2048]{1,0:T(8,128)(2,1)S(1)}, bf16[256,2048]{1,0:T(8,128)(2,1)}, u32[]{:S(2)}, u32[]{:S(2)}) %collective-permute-start.7) | collective-permute-done | bytes 1048608 | tf_op jit(solution)/shard_map/ppermute | solution.py:20
  387.4 189.2 %collective-permute-done.8 = bf16[512,2048]{1,0:T(8,128)(2,1)S(1)} collective-permute-done((bf16[512,2048]{1,0:T(8,128)(2,1)S(1)}, bf16[512,2048]{1,0:T(8,128)(2,1)S(1)}, u32[]{:S(2)}, u32[]{:S(2)}) %collective-permute-start.8) | collective-permute-done | bytes 2097184 | tf_op jit(solution)/shard_map/ppermute | solution.py:20
  580.3 23.1 %fusion.23 = f32[1024,3072]{1,0:T(8,128)} fusion(bf16[1024,2048]{1,0:T(8,128)(2,1)} %bitcast.259, bf16[1024,3072]{1,0:T(8,128)(2,1)} %collective-permute-done.4, bf16[1024,3072]{1,0:T(8,128)(2,1)} %maximum_select_fusion.1, pred[]{:T(512)S(6)} %eq.11), kind=kOutput, calls=%fused_computation.73 | convolution fusion | flops 12941524992 | bytes 29360128 | tf_op jit(solution)/shard_map/dot_general | solution.py:62
  686.2 22.7 %all-to-all-done.1 = bf16[4,64,1024]{2,1,0:T(8,128)(2,1)} async-done(((bf16[4,64,1024]{2,1,0:T(8,128)(2,1)}), bf16[4,64,1024]{2,1,0:T(8,128)(2,1)}, u32[]{:S(2)}, u32[]{:S(2)}) %all-to-all-start.1) | async-done | bytes 524320 | tf_op jit(solution)/shard_map/all_to_all | solution.py:100
  713.6 17.8 %collective-permute-done.21 = bf16[1,256,2048]{2,1,0:T(8,128)(2,1)} collective-permute-done((bf16[1,256,2048]{2,1,0:T(8,128)(2,1)}, bf16[1,256,2048]{2,1,0:T(8,128)(2,1)}, u32[]{:S(2)}, u32[]{:S(2)}) %collective-permute-start.21) | collective-permute-done | bytes 1048608 | tf_op jit(solution)/shard_map/ppermute | solution.py:71
  739.5 13.4 collective-permute-done.11
  766.0 36.0 %collective-permute-done.17 = bf16[256,2048]{1,0:T(8,128)(2,1)S(1)} collective-permute-done((bf16[256,2048]{1,0:T(8,128)(2,1)S(1)}, bf16[256,2048]{1,0:T(8,128)(2,1)S(1)}, u32[]{:S(2)}, u32[]{:S(2)}) %collective-permute-start.17) | collective-permute-done | bytes 1048608 | tf_op jit(solution)/shard_map/ppermute | solution.py:20
  806.1 96.1 %collective-permute-done.15 = bf16[1024,1024]{1,0:T(8,128)(2,1)S(1)} collective-permute-done((bf16[1024,1024]{1,0:T(8,128)(2,1)S(1)}, bf16[1024,1024]{1,0:T(8,128)(2,1)S(1)}, u32[]{:S(2)}, u32[]{:S(2)}) %collective-permute-start.15) | collective-permute-done | bytes 2097184 | tf_op jit(solution)/shard_map/ppermute | solution.py:20
  902.2 14.8 multiply_convert_fusion
  917.0 28.5 %collective-permute-done.18 = bf16[512,2048]{1,0:T(8,128)(2,1)S(1)} collective-permute-done((bf16[512,2048]{1,0:T(8,128)(2,1)S(1)}, bf16[512,2048]{1,0:T(8,128)(2,1)S(1)}, u32[]{:S(2)}, u32[]{:S(2)}) %collective-permute-start.18) | collective-permute-done | bytes 2097184 | tf_op jit(solution)/shard_map/ppermute | solution.py:20
  990.4 18.6 %collective-permute-done.24 = bf16[1,256,2048]{2,1,0:T(8,128)(2,1)S(1)} collective-permute-done((bf16[1,256,2048]{2,1,0:T(8,128)(2,1)S(1)}, bf16[1,256,2048]{2,1,0:T(8,128)(2,1)S(1)}, u32[]{:S(2)}, u32[]{:S(2)}) %collective-permute-start.24) | collective-permute-done | bytes 1048608 | tf_op jit(solution)/shard_map/ppermute | solution.py:71
  1009.8 21.3 %collective-permute-done.20 = bf16[1,256,2048]{2,1,0:T(8,128)(2,1)S(1)} collective-permute-done((bf16[1,256,2048]{2,1,0:T(8,128)(2,1)S(1)}, bf16[1,256,2048]{2,1,0:T(8,128)(2,1)S(1)}, u32[]{:S(2)}, u32[]{:S(2)}) %collective-permute-start.20) | collective-permute-done | bytes 1048608 | tf_op jit(solution)/shard_map/ppermute | solution.py:71
  1036.9 23.3 %collective-permute-done.25 = bf16[1,256,2048]{2,1,0:T(8,128)(2,1)S(1)} collective-permute-done((bf16[1,256,2048]{2,1,0:T(8,128)(2,1)S(1)}, bf16[1,256,2048]{2,1,0:T(8,128)(2,1)S(1)}, u32[]{:S(2)}, u32[]{:S(2)}) %collective-permute-start.25) | collective-permute-done | bytes 1048608 | tf_op jit(solution)/shard_map/ppermute | solution.py:71
  1131.0 16.0 convolution_convert_fusion
  1162.5 20.5 %fusion.22 = f32[1024,2048]{1,0:T(8,128)S(1)} fusion(bf16[1024,3072]{1,0:T(8,128)(2,1)} %copy-done.54, bf16[1024,3072]{1,0:T(8,128)(2,1)} %collective-permute-done.4, bf16[1024,3072]{1,0:T(8,128)(2,1)} %maximum_select_fusion.1, pred[]{:T(512)S(6)} %eq.11), kind=kOutput, calls=%fused_computation.72 | convolution fusion | flops 12941524992 | bytes 27262976 | tf_op jit(solution)/shard_map/dot_general | solution.py:62
  1200.9 21.9 %all-to-all-done.3 = bf16[4,64,1024]{2,1,0:T(8,128)(2,1)} async-done(((bf16[4,64,1024]{2,1,0:T(8,128)(2,1)}), bf16[4,64,1024]{2,1,0:T(8,128)(2,1)}, u32[]{:S(2)}, u32[]{:S(2)}) %all-to-all-start.3) | async-done | bytes 524320 | tf_op jit(solution)/shard_map/all_to_all | solution.py:100
  1234.8 131.6 %reduce-scatter.8.cloned.1.call-done = bf16[256,3072]{1,0:T(8,128)(2,1)} async-done(((bf16[2048,3072]{1,0:T(8,128)(2,1)}), bf16[256,3072]{1,0:T(8,128)(2,1)}) %reduce-scatter.8.cloned.1.call-update) | async-done | bytes 1572880 | tf_op jit(solution)/shard_map/reduce_scatter | solution.py:108
  1374.8 82.2 %reduce-scatter.10.cloned.1.call-done = bf16[128,2048]{1,0:T(8,128)(2,1)} async-done(((bf16[1024,2048]{1,0:T(8,128)(2,1)}), bf16[128,2048]{1,0:T(8,128)(2,1)}) %reduce-scatter.10.cloned.1.call-update) | async-done | bytes 524304 | tf_op jit(solution)/shard_map/reduce_scatter | solution.py:108
  1462.0 132.4 %reduce-scatter.16.cloned.1.call-done = f32[64,4]{1,0:T(8,128)} async-done(((f32[2048,4]{1,0:T(8,128)}), f32[64,4]{1,0:T(8,128)}) %reduce-scatter.16.cloned.1.call-update) | async-done | bytes 1040
  (407 shorter events, 354.3 us)
Async XLA Ops:
  36.0 35.8 %collective-permute-start.2 = (bf16[256,3072]{1,0:T(8,128)(2,1)S(1)}, bf16[256,3072]{1,0:T(8,128)(2,1)S(1)}, u32[]{:S(2)}, u32[]{:S(2)}) collective-permute-start(bf16[256,3072]{1,0:T(8,128)(2,1)S(1)} %bitcast.248), channel_id=1, source_target_pairs={{0,4},{4,0},{8,12},{12,8},{16,20},{20,16},{24,28},{28,24},{1,5},{5... | collective-permute-start | bytes 4718600 | tf_op jit(solution)/shard_map/ppermute | solution.py:20
  74.3 129.8 %collective-permute-start.3 = (bf16[512,3072]{1,0:T(8,128)(2,1)}, bf16[512,3072]{1,0:T(8,128)(2,1)}, u32[]{:S(2)}, u32[]{:S(2)}) collective-permute-start(bf16[512,3072]{1,0:T(8,128)(2,1)} %maximum_select_fusion.9), channel_id=1, source_target_pairs={{0,8},{4,12},{8,0},{12,4},{16,24},{20,28},{24,16},{28,20},{1,9},{5... | collective-permute-start | bytes 9437192 | tf_op jit(solution)/shard_map/ppermute | solution.py:20
  75.8 139.4 %collective-permute-start.5 = (bf16[128,2048]{1,0:T(8,128)(2,1)}, bf16[128,2048]{1,0:T(8,128)(2,1)S(1)}, u32[]{:S(2)}, u32[]{:S(2)}) collective-permute-start(bf16[128,2048]{1,0:T(8,128)(2,1)} %param.17), channel_id=1, source_target_pairs={{0,0},{1,4},{2,8},{3,12},{4,16},{5,20},{6,24},{7,28},{8,1},{9,5},{... | collective-permute-start | bytes 1572872 | tf_op jit(solution)/shard_map/ppermute | solution.py:146
  214.0 366.3 %collective-permute-start.4 = (bf16[1024,3072]{1,0:T(8,128)(2,1)}, bf16[1024,3072]{1,0:T(8,128)(2,1)}, u32[]{:S(2)}, u32[]{:S(2)}) collective-permute-start(bf16[1024,3072]{1,0:T(8,128)(2,1)} %maximum_select_fusion.1), channel_id=1, source_target_pairs={{0,16},{4,20},{8,24},{12,28},{16,0},{20,4},{24,8},{28,12},{1,17},{... | collective-permute-start | bytes 18874376 | tf_op jit(solution)/shard_map/ppermute | solution.py:20
  231.0 141.2 %collective-permute-start.7 = (bf16[256,2048]{1,0:T(8,128)(2,1)S(1)}, bf16[256,2048]{1,0:T(8,128)(2,1)}, u32[]{:S(2)}, u32[]{:S(2)}) collective-permute-start(bf16[256,2048]{1,0:T(8,128)(2,1)S(1)} %maximum_select_fusion.23), channel_id=1, source_target_pairs={{0,8},{4,12},{8,0},{12,4},{16,24},{20,28},{24,16},{28,20},{1,9},{5... | collective-permute-start | bytes 3145736 | tf_op jit(solution)/shard_map/ppermute | solution.py:20
  246.5 135.7 %collective-permute-start.1 = (bf16[2,256,2048]{2,1,0:T(8,128)(2,1)}, bf16[2,256,2048]{2,1,0:T(8,128)(2,1)}, u32[]{:S(2)}, u32[]{:S(2)}) collective-permute-start(bf16[2,256,2048]{2,1,0:T(8,128)(2,1)} %maximum_select_fusion.12), channel_id=1, source_target_pairs={{0,1},{1,0},{2,3},{3,2},{4,5},{5,4},{6,7},{7,6},{8,9},{9,8},{10,11... | collective-permute-start | bytes 6291464 | tf_op jit(solution)/shard_map/ppermute | solution.py:71
  374.6 202.0 %collective-permute-start.8 = (bf16[512,2048]{1,0:T(8,128)(2,1)S(1)}, bf16[512,2048]{1,0:T(8,128)(2,1)S(1)}, u32[]{:S(2)}, u32[]{:S(2)}) collective-permute-start(bf16[512,2048]{1,0:T(8,128)(2,1)S(1)} %maximum_select_fusion.14), channel_id=1, source_target_pairs={{0,16},{4,20},{8,24},{12,28},{16,0},{20,4},{24,8},{28,12},{1,17},{... | collective-permute-start | bytes 6291464 | tf_op jit(solution)/shard_map/ppermute | solution.py:20
  684.2 508.5 %reduce-scatter.12.cloned.1.call-start = ((), (), s32[]{:S(2)}) async-start(), calls=%async_computation.11 | async-start | bytes 4718592 | tf_op jit(solution)/shard_map/reduce_scatter | solution.py:108
  684.3 51.6 %collective-permute-start.16 = (bf16[128,2048]{1,0:T(8,128)(2,1)}, bf16[128,2048]{1,0:T(8,128)(2,1)}, u32[]{:S(2)}, u32[]{:S(2)}) collective-permute-start(bf16[128,2048]{1,0:T(8,128)(2,1)} %param.21), channel_id=1, source_target_pairs={{0,4},{4,0},{8,12},{12,8},{16,20},{20,16},{24,28},{28,24},{1,5},{5... | collective-permute-start | bytes 1572872 | tf_op jit(solution)/shard_map/ppermute | solution.py:20
  684.3 47.0 %collective-permute-start.21 = (bf16[1,256,2048]{2,1,0:T(8,128)(2,1)}, bf16[1,256,2048]{2,1,0:T(8,128)(2,1)}, u32[]{:S(2)}, u32[]{:S(2)}) collective-permute-start(bf16[1,256,2048]{2,1,0:T(8,128)(2,1)} %bitcast.42), channel_id=1, source_target_pairs={{0,2},{1,3},{2,0},{3,1},{4,6},{5,7},{6,4},{7,5},{8,10},{9,11},{10,... | collective-permute-start | bytes 3145736 | tf_op jit(solution)/shard_map/ppermute | solution.py:71
  712.1 40.8 %collective-permute-start.11 = (bf16[1,256,2048]{2,1,0:T(8,128)(2,1)S(1)}, bf16[1,256,2048]{2,1,0:T(8,128)(2,1)S(1)}, u32[]{:S(2)}, u32[]{:S(2)}) collective-permute-start(bf16[1,256,2048]{2,1,0:T(8,128)(2,1)S(1)} %fusion.127), channel_id=1, source_target_pairs={{0,2},{1,3},{2,0},{3,1},{4,6},{5,7},{6,4},{7,5},{8,10},{9,11},{10,... | collective-permute-start | bytes 3145736 | tf_op jit(solution)/shard_map/ppermute | solution.py:71
  734.0 69.3 %collective-permute-start.22 = (bf16[2,256,2048]{2,1,0:T(8,128)(2,1)S(1)}, bf16[2,256,2048]{2,1,0:T(8,128)(2,1)S(1)}, u32[]{:S(2)}, u32[]{:S(2)}) collective-permute-start(bf16[2,256,2048]{2,1,0:T(8,128)(2,1)S(1)} %maximum_select_fusion.19), channel_id=1, source_target_pairs={{0,1},{1,0},{2,3},{3,2},{4,5},{5,4},{6,7},{7,6},{8,9},{9,8},{10,11... | collective-permute-start | bytes 6291464 | tf_op jit(solution)/shard_map/ppermute | solution.py:71
  737.4 64.7 %collective-permute-start.17 = (bf16[256,2048]{1,0:T(8,128)(2,1)S(1)}, bf16[256,2048]{1,0:T(8,128)(2,1)S(1)}, u32[]{:S(2)}, u32[]{:S(2)}) collective-permute-start(bf16[256,2048]{1,0:T(8,128)(2,1)S(1)} %maximum_select_fusion.25), channel_id=1, source_target_pairs={{0,8},{4,12},{8,0},{12,4},{16,24},{20,28},{24,16},{28,20},{1,9},{5... | collective-permute-start | bytes 3145736 | tf_op jit(solution)/shard_map/ppermute | solution.py:20
  753.3 51.8 %collective-permute-start.12 = (bf16[2,256,2048]{2,1,0:T(8,128)(2,1)S(1)}, bf16[2,256,2048]{2,1,0:T(8,128)(2,1)S(1)}, u32[]{:S(2)}, u32[]{:S(2)}) collective-permute-start(bf16[2,256,2048]{2,1,0:T(8,128)(2,1)S(1)} %maximum_select_fusion.15), channel_id=1, source_target_pairs={{0,1},{1,0},{2,3},{3,2},{4,5},{5,4},{6,7},{7,6},{8,9},{9,8},{10,11... | collective-permute-start | bytes 6291464 | tf_op jit(solution)/shard_map/ppermute | solution.py:71
  762.8 139.4 %collective-permute-start.15 = (bf16[1024,1024]{1,0:T(8,128)(2,1)S(1)}, bf16[1024,1024]{1,0:T(8,128)(2,1)S(1)}, u32[]{:S(2)}, u32[]{:S(2)}) collective-permute-start(bf16[1024,1024]{1,0:T(8,128)(2,1)S(1)} %maximum_select_fusion.17), channel_id=1, source_target_pairs={{0,16},{4,20},{8,24},{12,28},{16,0},{20,4},{24,8},{28,12},{1,17},{... | collective-permute-start | bytes 6291464 | tf_op jit(solution)/shard_map/ppermute | solution.py:20
  803.0 142.4 %collective-permute-start.18 = (bf16[512,2048]{1,0:T(8,128)(2,1)S(1)}, bf16[512,2048]{1,0:T(8,128)(2,1)S(1)}, u32[]{:S(2)}, u32[]{:S(2)}) collective-permute-start(bf16[512,2048]{1,0:T(8,128)(2,1)S(1)} %maximum_select_fusion.18), channel_id=1, source_target_pairs={{0,16},{4,20},{8,24},{12,28},{16,0},{20,4},{24,8},{28,12},{1,17},{... | collective-permute-start | bytes 6291464 | tf_op jit(solution)/shard_map/ppermute | solution.py:20
  964.2 234.6 %reduce-scatter.14.cloned.1.call-start = ((), (), s32[]{:S(2)}) async-start(), calls=%async_computation.12 | async-start | bytes 4718592 | tf_op jit(solution)/shard_map/reduce_scatter | solution.py:108
  988.9 42.2 %collective-permute-start.20 = (bf16[1,256,2048]{2,1,0:T(8,128)(2,1)S(1)}, bf16[1,256,2048]{2,1,0:T(8,128)(2,1)S(1)}, u32[]{:S(2)}, u32[]{:S(2)}) collective-permute-start(bf16[1,256,2048]{2,1,0:T(8,128)(2,1)S(1)} %dynamic-slice_convert_fusion.3), channel_id=1, source_target_pairs={{0,2},{1,3},{2,0},{3,1},{4,6},{5,7},{6,4},{7,5},{8,10},{9,11},{10,... | collective-permute-start | bytes 3145736 | tf_op jit(solution)/shard_map/ppermute | solution.py:71
  1068.6 297.8 %reduce-scatter.8.cloned.1.call-start = ((), (), s32[]{:S(2)}) async-start(), calls=%async_computation.9 | async-start | bytes 14155776 | tf_op jit(solution)/shard_map/reduce_scatter | solution.py:108
  1147.0 310.0 %reduce-scatter.10.cloned.1.call-start = ((), (), s32[]{:S(2)}) async-start(), calls=%async_computation.10 | async-start | bytes 4718592 | tf_op jit(solution)/shard_map/reduce_scatter | solution.py:108
  1191.5 36.9 %collective-permute-start.28 = (bf16[1,256,2048]{2,1,0:T(8,128)(2,1)}, bf16[1,256,2048]{2,1,0:T(8,128)(2,1)}, u32[]{:S(2)}, u32[]{:S(2)}) collective-permute-start(bf16[1,256,2048]{2,1,0:T(8,128)(2,1)} %dynamic-slice_convert_fusion.1), channel_id=1, source_target_pairs={{0,2},{1,3},{2,0},{3,1},{4,6},{5,7},{6,4},{7,5},{8,10},{9,11},{10,... | collective-permute-start | bytes 3145736 | tf_op jit(solution)/shard_map/ppermute | solution.py:71
  1196.8 397.5 %reduce-scatter.16.cloned.1.call-start = ((), (), s32[]{:S(2)}) async-start(), calls=%async_computation.13 | async-start | bytes 1081344
  1366.5 232.4 %all-to-all-start.2 = ((bf16[4,64,3072]{2,1,0:T(8,128)(2,1)}), bf16[4,64,3072]{2,1,0:T(8,128)(2,1)}, u32[]{:S(2)}, u32[]{:S(2)}) async-start(bf16[4,64,3072]{2,1,0:T(8,128)(2,1)} %bitcast.281), calls=%async_computation.3 | async-start | bytes 3145728 | tf_op jit(solution)/shard_map/all_to_all | solution.py:100
  1457.0 140.7 %collective-permute-start.29 = (bf16[128,2048]{1,0:T(8,128)(2,1)}, bf16[128,2048]{1,0:T(8,128)(2,1)S(1)}, u32[]{:S(2)}, u32[]{:S(2)}) collective-permute-start(bf16[128,2048]{1,0:T(8,128)(2,1)} %reduce-scatter.10.cloned.1.call-done), channel_id=1, source_target_pairs={{0,0},{4,1},{8,2},{12,3},{16,4},{20,5},{24,6},{28,7},{1,8},{5,9},{... | collective-permute-start | bytes 1572872 | tf_op jit(solution)/shard_map/ppermute | solution.py:223
  (102 other events, 2660.4 us)
Sparse Core Ops, SparseCore 0:
  964.3 86.8 reduce-scatter.11
  1068.8 87.0 reduce-scatter.13
  1159.4 206.9 reduce-scatter.7
  1369.9 87.0 reduce-scatter.9
  1459.8 134.5 reduce-scatter.15
